TPU v7x, 32 devices: a whole 2x2x4 slice. The times are simulated.
32 devices in a mesh: fsdp: 4 (over z), ctx: 4 (over y, x), tp: 2 (over core).
Axes of the slice: x: 2, y: 2, z: 4, core: 2. Of those that a mesh axis runs over, the one named last changes fastest.
Arguments:
- tokens: bfloat16 [4096, 1024], P(('fsdp', 'ctx')), may hold values from -6 to 6
- lengths: int32 [4, 4], P('fsdp'), may hold values from 1 to 959, as said below
- norm_gain: bfloat16 [1024], P('fsdp'), may hold values from 0.5 to 1.5
- qkv_weight: bfloat16 [3, 1024, 1024], P(None, 'fsdp', 'tp'), may hold values from -0.1875 to 0.1875
- beta_weight: bfloat16 [1024, 8], P('fsdp', 'tp'), may hold values from -0.1875 to 0.1875
- conv_weight: bfloat16 [3, 4, 8, 128], P(None, None, 'tp', 'fsdp'), may hold values from -3 to 3
- head_gain: bfloat16 [128], P('fsdp'), may hold values from 0.5 to 1.5
- out_weight: bfloat16 [1024, 1024], P('tp', 'fsdp'), may hold values from -0.1875 to 0.1875
- mlp_gain: bfloat16 [1024], P('fsdp'), may hold values from 0.5 to 1.5
- gate_up_weight: bfloat16 [2, 1024, 2816], P(None, 'fsdp', 'tp'), may hold values from -0.1875 to 0.1875
- down_weight: bfloat16 [2816, 1024], P('tp', 'fsdp'), may hold values from -0.15625 to 0.15625
- cotangent: bfloat16 [4096, 1024], P(('fsdp', 'ctx')), may hold values from -6 to 6
Outputs:
- layer_out: bfloat16 [4096, 1024], P(('fsdp', 'ctx'))
- input_grad: float32 [4096, 1024], P(('fsdp', 'ctx'))
- norm_gain_grad: float32 [1024], P('fsdp')
- qkv_grad: float32 [3, 1024, 1024], P(None, 'fsdp', 'tp')
- beta_grad: float32 [1024, 8], P('fsdp', 'tp')
- conv_grad: float32 [3, 4, 8, 128], P(None, None, 'tp', 'fsdp')
- head_gain_grad: float32 [128], P('fsdp')
- out_grad: float32 [1024, 1024], P('tp', 'fsdp')
- mlp_gain_grad: float32 [1024], P('fsdp')
- gate_up_grad: float32 [2, 1024, 2816], P(None, 'fsdp', 'tp')
- down_grad: float32 [2816, 1024], P('tp', 'fsdp')
- rms: float32 [5], replicated
Inputs may be any that keep to these rules, and one draw needn't show every extreme that they name: Row g lists the 4 sequence lengths of stream g in order; they sum to at most 1024, the remaining slots at the end are padding. The second sequence of each stream ends at slot 960, so it includes a slot of the first and of the last of its 4 blocks of 256 slots.
All inputs are finite; a program needn't handle non-finite values.
Results may differ from a plain program's by a relative error of at most 0.012.
The roundings to bfloat16 on the way count: a program that leaves them out, or rounds other values in their place, can miss the bound.
Values may be sent and summed in bfloat16 or wider, within the bound.
No kernel may reach another device: no remote copies, remote signals or barrier semaphores. Data moves between devices by JAX's collectives and lax.ppermute only.
A program may use at most 128 MiB of HBM per device.

v0:
```python
import jax
import jax.numpy as jnp
from jax import lax
from jax.sharding import PartitionSpec as P

D = 1024
HD = 128
C = 64
CONV = 4
PRECISE = lax.Precision.HIGHEST
NORM_EPS = 1e-06


def passed_along(value, axis, steps):
    count = lax.axis_size(axis)
    leading, last = (max(0, -steps), min(count, count - steps))
    return lax.ppermute(value, axis, [(source, source + steps) for source in range(leading, last)])


def product(form, left, right):
    return jnp.einsum(form, left, right, precision=PRECISE)


def rounded(values):
    return lax.optimization_barrier(values.astype(jnp.bfloat16)).astype(jnp.float32)


def rms_norm(values, gain):
    return values * lax.rsqrt(jnp.mean(values * values, -1, keepdims=True) + NORM_EPS) * gain


def norm_back(values, gain, grad):
    ratio = lax.rsqrt(jnp.mean(values * values, -1, keepdims=True) + NORM_EPS)
    scaled = values * ratio
    weighted = grad * gain
    value_grad = ratio * (weighted - scaled * jnp.mean(weighted * scaled, -1, keepdims=True))
    gain_grad = jnp.sum((grad * scaled).reshape(-1, values.shape[-1]), 0)
    return (value_grad, gain_grad)


def l2_norm(values):
    return values * lax.rsqrt(jnp.sum(values * values, -1, keepdims=True) + NORM_EPS)


def seq_layout(lengths_row, first, row_count):
    ends = jnp.cumsum(lengths_row)
    places = first + jnp.arange(row_count, dtype=jnp.int32)
    passed = ends[None, :] <= places[:, None]
    begins = jnp.max(jnp.where(passed, ends[None, :], 0), -1)
    seg_ids = jnp.sum(passed.astype(jnp.int32), -1)
    valid = (places < ends[-1]).astype(jnp.float32)
    resets = places == begins
    offsets = places[:, None] - (CONV - 1) + jnp.arange(CONV, dtype=jnp.int32)[None, :]
    taps = (offsets >= begins[:, None]).astype(jnp.float32)
    return (seg_ids, resets, valid, taps)


def block_masks(seg_ids, resets):
    seg_blocks = seg_ids.reshape(-1, C)
    same_seq = (seg_blocks[:, :, None] == seg_blocks[:, None, :]).astype(jnp.float32)
    reset_count = jnp.cumsum(resets.reshape(-1, C).astype(jnp.int32), -1)
    carried = (reset_count == 0).astype(jnp.float32)
    return (same_seq, carried)


def conv_heads(extended, conv_taps, taps):
    row_count = taps.shape[0]
    total = jnp.zeros((row_count,) + extended.shape[1:], jnp.float32)
    for offset in range(CONV):
        total = (
            total
            + extended[offset : offset + row_count]
            * conv_taps[:, offset][None]
            * taps[:, offset][:, None, None]
        )
    activated = jax.nn.silu(total)
    head_count = extended.shape[2] // HD
    split_rows = activated.reshape(row_count, 3, head_count, HD)
    return (l2_norm(split_rows[:, 0]), l2_norm(split_rows[:, 1]), split_rows[:, 2])


def to_blocks(values):
    return values.reshape(values.shape[0] // C, C, values.shape[1], values.shape[2]).transpose(
        2, 0, 1, 3
    )


def beta_blocks(values):
    return values.reshape(values.shape[0] // C, C, values.shape[1]).transpose(2, 0, 1)


def from_blocks(values):
    return values.transpose(1, 2, 0, 3).reshape(-1, values.shape[0], values.shape[3])


def unit_inverse(lower):
    size_now = lower.shape[-1]
    identity = jnp.eye(size_now, dtype=jnp.float32)
    inverse = identity - lower
    power = lower
    span = 2
    while span < size_now:
        power = product("...ij,...jk->...ik", power, power)
        inverse = product("...ij,...jk->...ik", inverse, identity + power)
        span = span * 2
    return inverse


def block_terms(queries, key_rows, value_rows, beta_rows, same_seq, carried):
    wide = key_rows.shape[-1]
    last_seg = same_seq[:, -1, :]
    key_gram = product("hncd,hnmd->hncm", key_rows, key_rows)
    lower = jnp.tril(beta_rows[..., :, None] * key_gram * same_seq, -1)
    inverse = unit_inverse(lower)
    stacked = beta_rows[..., None] * jnp.concatenate([key_rows, value_rows], -1)
    solved = product("hncm,hnmd->hncd", inverse, stacked)
    w_part = solved[..., :wide]
    u_part = solved[..., wide:]
    query_key = jnp.tril(product("hncd,hnmd->hncm", queries, key_rows) * same_seq)
    keep_all = carried[:, -1]
    trans = keep_all[:, None, None] * jnp.eye(wide, dtype=jnp.float32) - product(
        "hnci,hncj->hnij", w_part * (carried * last_seg)[..., None], key_rows
    )
    push = product("hnci,hncj->hnij", u_part * last_seg[..., None], key_rows)
    return (w_part, u_part, query_key, queries, trans, push)


def run_blocks(terms, carried, start_state):
    sequenced = tuple((jnp.moveaxis(piece, 1, 0) for piece in terms)) + (carried,)

    def advance(state, pieces):
        w_now, u_now, qk_now, q_now, trans_now, push_now, carry_now = pieces
        carry_col = carry_now[None, :, None]
        from_state = product("hcd,hvd->hcv", w_now, state)
        fresh = u_now - carry_col * from_state
        output = carry_col * product("hcd,hvd->hcv", q_now, state) + product(
            "hcm,hmv->hcv", qk_now, fresh
        )
        following = product("hvk,hkj->hvj", state, trans_now) + push_now
        return (following, output)

    final_state, outputs = lax.scan(advance, start_state, sequenced)
    return (jnp.moveaxis(outputs, 0, 1), final_state)


def join_maps(earlier, later):
    return (
        product("hik,hkj->hij", earlier[0], later[0]),
        product("hvk,hkj->hvj", earlier[1], later[0]) + later[1],
    )


def row_total(values, valid):
    return jnp.sum(valid * jnp.sum(values * values, -1))


def local(
    tokens,
    lengths,
    norm_gain,
    qkv_weight,
    beta_weight,
    conv_weight,
    head_gain,
    out_weight,
    mlp_gain,
    gate_up_weight,
    down_weight,
    cotangent,
):
    row_count = tokens.shape[0]
    ctx_count = lax.axis_size("ctx")
    fsdp_count = lax.axis_size("fsdp")
    seg_ids, resets, valid, taps = seq_layout(
        lengths[0], lax.axis_index("ctx") * row_count, row_count
    )
    same_seq, carried = block_masks(seg_ids, resets)
    gathered = (
        lax.all_gather(norm_gain, "fsdp", axis=0, tiled=True),
        lax.all_gather(qkv_weight, "fsdp", axis=1, tiled=True),
        lax.all_gather(beta_weight, "fsdp", axis=0, tiled=True),
        lax.all_gather(conv_weight, "fsdp", axis=3, tiled=True),
        lax.all_gather(head_gain, "fsdp", axis=0, tiled=True),
        lax.all_gather(out_weight, "fsdp", axis=1, tiled=True),
        lax.all_gather(mlp_gain, "fsdp", axis=0, tiled=True),
        lax.all_gather(gate_up_weight, "fsdp", axis=1, tiled=True),
        lax.all_gather(down_weight, "fsdp", axis=1, tiled=True),
    )
    (
        first_gain,
        qkv_full,
        beta_full,
        conv_full,
        head_full,
        out_full,
        second_gain,
        gate_up_full,
        down_full,
    ) = gathered
    heads_local = beta_full.shape[1]
    width_local = qkv_full.shape[2]
    x_wide = tokens.astype(jnp.float32)
    first_f = first_gain.astype(jnp.float32)
    second_f = second_gain.astype(jnp.float32)
    head_f = head_full.astype(jnp.float32)
    normed_in = rms_norm(x_wide, first_f).astype(jnp.bfloat16)
    projected = jnp.einsum(
        "td,idk->tik", normed_in, qkv_full, preferred_element_type=jnp.float32
    ).astype(jnp.bfloat16)
    beta_rows = jax.nn.sigmoid(jnp.dot(normed_in, beta_full, preferred_element_type=jnp.float32))
    rim_rows = passed_along(projected[row_count - (CONV - 1) :], "ctx", 1)
    extended = jnp.concatenate([rim_rows, projected], 0).astype(jnp.float32)
    conv_local = conv_full.reshape(3, CONV, width_local).astype(jnp.float32)

    def conv_part(ext_rows, conv_taps):
        return conv_heads(ext_rows, conv_taps, taps)

    (query_raw, key_raw, value_raw), conv_pull = jax.vjp(conv_part, extended, conv_local)
    queries = rounded(query_raw)
    key_rows = rounded(key_raw)
    value_rows = rounded(value_raw)

    def prepare(query_in, key_in, value_in, beta_in):
        return block_terms(
            to_blocks(query_in) * HD ** (-0.5),
            to_blocks(key_in),
            to_blocks(value_in),
            beta_blocks(beta_in),
            same_seq,
            carried,
        )

    terms, prepare_pull = jax.vjp(prepare, queries, key_rows, value_rows, beta_rows)
    identity = jnp.broadcast_to(jnp.eye(HD, dtype=jnp.float32), (heads_local, HD, HD))
    empty_state = jnp.zeros((heads_local, HD, HD), jnp.float32)

    def compose(accum, pieces):
        return (join_maps(accum, pieces), None)

    (device_map, device_shift), ignored = lax.scan(
        compose,
        (identity, empty_state),
        (jnp.moveaxis(terms[4], 1, 0), jnp.moveaxis(terms[5], 1, 0)),
    )
    incoming = empty_state
    for repeat in range(ctx_count - 1):
        incoming = passed_along(
            product("hvk,hkj->hvj", incoming, device_map) + device_shift, "ctx", 1
        )

    def run_part(term_in, state_in):
        return run_blocks(term_in, carried, state_in)

    (out_blocks, ignored_state), run_pull = jax.vjp(run_part, terms, incoming)
    mixed_out = from_blocks(out_blocks)
    head_normed = rms_norm(mixed_out, head_f).reshape(row_count, width_local).astype(jnp.bfloat16)
    attn_rows = (
        lax.psum(jnp.dot(head_normed, out_full, preferred_element_type=jnp.float32), "tp")
        * valid[:, None]
    )
    middle = x_wide + attn_rows
    normed_mid = rms_norm(middle, second_f).astype(jnp.bfloat16)
    gate_up = jnp.einsum(
        "td,idf->tif", normed_mid, gate_up_full, preferred_element_type=jnp.float32
    )
    gate_rows = gate_up[:, 0]
    up_rows = gate_up[:, 1]
    activated = (jax.nn.silu(gate_rows) * up_rows).astype(jnp.bfloat16)
    ffn_rows = (
        lax.psum(jnp.dot(activated, down_full, preferred_element_type=jnp.float32), "tp")
        * valid[:, None]
    )
    result = middle + ffn_rows
    stat_sums = jnp.stack(
        [
            row_total(x_wide, valid),
            row_total(attn_rows, valid),
            row_total(middle, valid),
            row_total(ffn_rows, valid),
            row_total(result, valid),
            jnp.sum(valid),
        ]
    )
    out_cot = cotangent.astype(jnp.float32)
    ffn_back = (out_cot * valid[:, None]).astype(jnp.bfloat16)
    down_grad = jnp.einsum("tf,td->fd", activated, ffn_back, preferred_element_type=jnp.float32)
    act_grad = jnp.einsum("td,fd->tf", ffn_back, down_full, preferred_element_type=jnp.float32)
    gate_sig = jax.nn.sigmoid(gate_rows)
    up_grad = act_grad * gate_rows * gate_sig
    gate_grad = act_grad * up_rows * gate_sig * (1.0 + gate_rows * (1.0 - gate_sig))
    gate_up_back = jnp.stack([gate_grad, up_grad], 1).astype(jnp.bfloat16)
    gate_up_grad = jnp.einsum(
        "td,tif->idf", normed_mid, gate_up_back, preferred_element_type=jnp.float32
    )
    mid_part = jnp.einsum(
        "tif,idf->td", gate_up_back, gate_up_full, preferred_element_type=jnp.float32
    )
    mid_grad = lax.psum(mid_part, "tp")
    middle_norm_grad, second_gain_grad = norm_back(middle, second_f, mid_grad)
    middle_grad = out_cot + middle_norm_grad
    attn_back = (middle_grad * valid[:, None]).astype(jnp.bfloat16)
    out_grad = jnp.einsum("tk,td->kd", head_normed, attn_back, preferred_element_type=jnp.float32)
    head_in_grad = jnp.einsum(
        "td,kd->tk", attn_back, out_full, preferred_element_type=jnp.float32
    ).reshape(row_count, heads_local, HD)
    mixed_grad, head_gain_part = norm_back(mixed_out, head_f, head_in_grad)
    mixed_blocks = to_blocks(mixed_grad)

    def state_part(state_in):
        return run_blocks(terms, carried, state_in)[0]

    ignored_out, state_pull = jax.vjp(state_part, incoming)
    local_state = state_pull(mixed_blocks)[0]
    map_turned = jnp.swapaxes(device_map, 1, 2)
    outgoing = empty_state
    for repeat in range(ctx_count - 1):
        outgoing = passed_along(
            local_state + product("hvk,hkj->hvj", outgoing, map_turned), "ctx", -1
        )
    term_grads, ignored_grad = run_pull((mixed_blocks, outgoing))
    query_grad, key_grad, value_grad, beta_row_grad = prepare_pull(term_grads)
    logit_grad = (beta_row_grad * beta_rows * (1.0 - beta_rows)).astype(jnp.bfloat16)
    ext_grad, conv_grad_flat = conv_pull((query_grad, key_grad, value_grad))
    back_rim = passed_along(ext_grad[: CONV - 1], "ctx", -1)
    proj_grad = ext_grad[CONV - 1 :] + jnp.concatenate(
        [jnp.zeros((row_count - (CONV - 1),) + back_rim.shape[1:], jnp.float32), back_rim], 0
    )
    proj_back = proj_grad.astype(jnp.bfloat16)
    qkv_grad = jnp.einsum("td,tik->idk", normed_in, proj_back, preferred_element_type=jnp.float32)
    beta_grad = jnp.einsum("td,th->dh", normed_in, logit_grad, preferred_element_type=jnp.float32)
    in_part = jnp.einsum(
        "tik,idk->td", proj_back, qkv_full, preferred_element_type=jnp.float32
    ) + jnp.einsum("th,dh->td", logit_grad, beta_full, preferred_element_type=jnp.float32)
    in_grad, head_gain_grad = lax.psum((in_part, head_gain_part), "tp")
    x_norm_grad, first_gain_grad = norm_back(x_wide, first_f, in_grad)
    input_grad = middle_grad + x_norm_grad
    stat_rows = jnp.broadcast_to(stat_sums[None, :], (fsdp_count, stat_sums.shape[0]))
    conv_grad = conv_grad_flat.reshape(3, CONV, heads_local, HD)
    shares = (
        lax.psum_scatter(first_gain_grad, "fsdp", scatter_dimension=0, tiled=True),
        lax.psum_scatter(qkv_grad, "fsdp", scatter_dimension=1, tiled=True),
        lax.psum_scatter(beta_grad, "fsdp", scatter_dimension=0, tiled=True),
        lax.psum_scatter(conv_grad, "fsdp", scatter_dimension=3, tiled=True),
        lax.psum_scatter(head_gain_grad, "fsdp", scatter_dimension=0, tiled=True),
        lax.psum_scatter(out_grad, "fsdp", scatter_dimension=1, tiled=True),
        lax.psum_scatter(second_gain_grad, "fsdp", scatter_dimension=0, tiled=True),
        lax.psum_scatter(gate_up_grad, "fsdp", scatter_dimension=1, tiled=True),
        lax.psum_scatter(down_grad, "fsdp", scatter_dimension=1, tiled=True),
        lax.psum_scatter(stat_rows, "fsdp", scatter_dimension=0, tiled=True),
    )
    totals = lax.psum(
        (
            shares[0],
            shares[1],
            shares[2],
            shares[3],
            shares[4],
            shares[5],
            shares[6],
            shares[7],
            shares[8],
            shares[9],
        ),
        "ctx",
    )
    stat_total = totals[9][0]
    rms = jnp.sqrt(stat_total[:5] / (stat_total[5] * D))
    return (
        result.astype(jnp.bfloat16),
        input_grad,
        totals[0],
        totals[1],
        totals[2],
        totals[3],
        totals[4],
        totals[5],
        totals[6],
        totals[7],
        totals[8],
        rms,
    )


def solution(mesh):
    return jax.shard_map(
        local,
        mesh=mesh,
        in_specs=(
            P(("fsdp", "ctx"), None),
            P("fsdp", None),
            P("fsdp"),
            P(None, "fsdp", "tp"),
            P("fsdp", "tp"),
            P(None, None, "tp", "fsdp"),
            P("fsdp"),
            P("tp", "fsdp"),
            P("fsdp"),
            P(None, "fsdp", "tp"),
            P("tp", "fsdp"),
            P(("fsdp", "ctx"), None),
        ),
        out_specs=(
            P(("fsdp", "ctx"), None),
            P(("fsdp", "ctx"), None),
            P("fsdp"),
            P(None, "fsdp", "tp"),
            P("fsdp", "tp"),
            P(None, None, "tp", "fsdp"),
            P("fsdp"),
            P("tp", "fsdp"),
            P("fsdp"),
            P(None, "fsdp", "tp"),
            P("tp", "fsdp"),
            P(),
        ),
        check_vma=False,
    )
```

profile of v0, /device:TPU:0, one launch (start us, length us, event | category | flops | bytes accessed | tf_op | source)
XLA Modules:
  0.0 1154.2 jit_solution(13363397626016956386)
XLA Ops:
  10.7 12.6 %all-gather = bf16[4,1,256]{2,1,0:T(2,128)(2,1)S(1)} all-gather(bf16[1,1,256]{2,1,0:T(2,128)(2,1)S(1)} %reshape.331), channel_id=1, replica_groups=mesh['fsdp'=4,'ctx'=4,'tp'=2] {'fsdp'}, dimensions={0}, use_global_device_ids=true | all-gather | bytes 2560 | tf_op jit(solution)/shard_map/all_gather | solution.py:179
  24.0 17.8 %all_gather.30 = bf16[3,4,4,128]{2,1,0,3:T(4,128)(2,1)S(1)} all-gather(bf16[3,4,4,32]{2,1,0,3:T(4,128)(2,1)S(1)} %copy.589), channel_id=1, replica_groups=mesh['fsdp'=4,'ctx'=4,'tp'=2] {'fsdp'}, dimensions={3}, use_global_device_ids=true | all-gather | bytes 15360 | tf_op jit(solution)/shard_map/all_gather | solution.py:182
  42.4 12.2 %all_gather.28 = bf16[1024,4]{0,1:T(4,128)(2,1)S(1)} all-gather(bf16[256,4]{0,1:T(4,128)(2,1)S(1)} %copy-done.132), channel_id=1, replica_groups=mesh['fsdp'=4,'ctx'=4,'tp'=2] {'fsdp'}, dimensions={0}, use_global_device_ids=true | all-gather | bytes 10240 | tf_op jit(solution)/shard_map/all_gather | solution.py:181
  57.8 11.3 all-reduce.14
  70.2 11.6 %all-gather.7.cloned.1.call-done = bf16[3,1024,512]{2,1,0:T(8,128)(2,1)} async-done(((bf16[3,256,512]{2,1,0:T(8,128)(2,1)}), bf16[3,1024,512]{2,1,0:T(8,128)(2,1)}) %all-gather.7.cloned.1.call-update) | async-done | bytes 3145744 | tf_op jit(solution)/shard_map/all_gather | solution.py:180
  81.8 2.9 convolution_convert_fusion
  84.8 3.4 collective-permute-start
  89.8 2.9 fusion.96
  92.7 2.9 reshape.310
  95.6 2.1 fusion.237
  107.5 2.1 copy.603
  118.5 2.5 convolution_bitcast_fusion.12
  121.0 2.5 copy.609
  123.5 2.0 fusion.101
  127.2 13.8 %while.85 = (s32[]{:T(128)}, f32[4,128,128]{1,2,0:T(8,128)S(1)}, f32[4,128,128]{1,2,0:T(8,128)}, f32[4,4,128,128]{2,3,1,0:T(8,128)S(1)}, f32[4,4,128,128]{2,3,1,0:T(8,128)}, /*index=5*/s32[]{:T(128)}, s32[]{:T(128)}) while((s32[]{:T(128)}, f32[4,128,128]{1,2,0:T(8,128)S(1)}, f32[4,128,128]{1,2,0:T(8,128)}, ...), condition=%wide.region_7.8_spmd.clone, body=%wide.region_6.7_spmd.clone.sunk | while | flops 201457664 | bytes 2884699 | solution.py:240
  128.2 2.0 fusion.424
  131.6 2.0 fusion.424
  135.1 2.0 fusion.424
  138.5 2.0 fusion.424
  144.7 4.2 collective-permute-start.1
  150.2 3.1 collective-permute-done.1
  154.0 4.4 collective-permute-start.2
  159.3 2.9 collective-permute-done.2
  162.9 5.9 collective-permute-start.3
  173.9 33.4 %while.82 = (s32[]{:T(128)}, f32[4,128,128]{1,2,0:T(8,128)}, f32[4,4,64,128]{3,2,1,0:T(8,128)}, f32[4,4,128,128]{2,3,1,0:T(8,128)S(1)}, f32[4,1,64,1]{2,3,1,0:T(...) while((s32[]{:T(128)}, f32[4,128,128]{1,2,0:T(8,128)}, ...), condition=%wide.region_10.11_spmd, body=%wide.region_9.10_spmd.sunk | while | flops 226689024 | bytes 3937937 | solution.py:142
  180.1 2.1 fusion.401
  188.4 2.1 fusion.401
  196.8 2.1 fusion.401
  205.1 2.1 fusion.401
  212.4 2.7 fusion.248
  216.9 9.6 all-gather.1
  227.7 9.6 all-reduce.28.cloned.1.call-done
  239.1 107.7 %all-gather.11.cloned.1.call-done = bf16[2,1024,1408]{2,1,0:T(8,128)(2,1)} async-done(((bf16[2,256,1408]{2,1,0:T(8,128)(2,1)}), bf16[2,1024,1408]{2,1,0:T(8,128)(2,1)}) %all-gather.11.cloned.1.call-update) | async-done | bytes 5767184 | tf_op jit(solution)/shard_map/all_gather | solution.py:186
  346.8 5.9 fusion.207
  352.7 53.0 %all-gather.13.cloned.1.call-done = bf16[1408,1024]{1,0:T(8,128)(2,1)} async-done(((bf16[1408,256]{1,0:T(8,128)(2,1)}), bf16[1408,1024]{1,0:T(8,128)(2,1)}) %all-gather.13.cloned.1.call-update) | async-done | bytes 2883600 | tf_op jit(solution)/shard_map/all_gather | solution.py:187
  405.7 4.4 fusion.133
  412.2 2.7 convolution_bitcast_fusion.13
  414.9 2.8 while.83
  417.7 2.0 copy.634
  421.6 12.9 %all-reduce.34.cloned.1.call-done = (f32[256,1024]{1,0:T(8,128)}, f32[256,1024]{1,0:T(8,128)}) async-done(((f32[256,1024]{1,0:T(8,128)}, f32[256,1024]{1,0:T(8,128)}), (f32[256,1024]{1,0:T(8,128)}, f32[256,1024]{1,0:T(8,128)})) %all-reduce.34.cloned.1.call-update) | async-done | bytes 2097168 | tf_op jit(solution)/shard_map/psum | solution.py:270
  434.5 3.9 multiply_reduce_fusion.4
  441.6 2.0 fusion.226
  448.6 22.0 %while.86 = (s32[]{:T(128)}, f32[4,128,128]{1,2,0:T(8,128)}, f32[4,4,128,128]{3,2,1,0:T(8,128)}, f32[4,1,64,1]{2,3,1,0:T(1,128)S(1)}, f32[4,4,64,128]{3,2,1,0:T(...) while((s32[]{:T(128)}, f32[4,128,128]{1,2,0:T(8,128)}, ...), condition=%wide.region_21.22_spmd.clone, body=%wide.region_20.21_spmd.clone.sunk | while | flops 226787328 | bytes 2756239 | solution.py:142
  475.1 9.1 collective-permute-done.4
  486.8 9.3 collective-permute-done.5
  498.5 3.5 fusion.195
  502.1 5.2 collective-permute-done.6
  513.9 51.4 %while.84 = (s32[]{:T(128)}, f32[4,128,128]{1,2,0:T(8,128)S(1)}, f32[4,4,64,128]{3,2,0,1:T(8,128)}, f32[4,4,64,128]{3,2,0,1:T(8,128)}, f32[4,4,64,64]{2,3,1,0:T(...) while((s32[]{:T(128)}, f32[4,128,128]{1,2,0:T(8,128)S(1)}, ...), condition=%wide.region_23.24_spmd, body=%wide.region_22.23_spmd.sunk | while | flops 453312512 | bytes 9840861 | solution.py:142
  594.6 2.1 fusion.126
  606.9 4.2 collective-permute-done.7
  611.2 3.7 convolution_bitcast_fusion.10
  616.1 8.1 convolution_bitcast_fusion.9
  629.4 4.2 fusion.102
  633.7 93.4 %reduce-scatter.11.cloned.1.call-done = f32[3,256,512]{1,2,0:T(8,128)} async-done(((f32[3,1024,512]{1,2,0:T(8,128)}), f32[3,256,512]{1,2,0:T(8,128)}) %reduce-scatter.11.cloned.1.call-update) | async-done | bytes 1572880 | tf_op jit(solution)/shard_map/reduce_scatter | solution.py:341
  727.1 197.8 %reduce-scatter.15.cloned.1.call-done = f32[2,256,1408]{1,2,0:T(8,128)} async-done(((f32[2,1024,1408]{1,2,0:T(8,128)}), f32[2,256,1408]{1,2,0:T(8,128)}) %reduce-scatter.15.cloned.1.call-update) | async-done | bytes 2883600 | tf_op jit(solution)/shard_map/reduce_scatter | solution.py:347
  927.2 4.0 stack.42
  931.4 19.1 %reduce-scatter.19.cloned.1.call-done = f32[256,4]{1,0:T(8,128)} async-done(((f32[1024,4]{1,0:T(8,128)}), f32[256,4]{1,0:T(8,128)}) %reduce-scatter.19.cloned.1.call-update) | async-done | bytes 4112
  951.5 19.1 %reduce-scatter.21.cloned.1.call-done = f32[32,48]{1,0:T(8,128)} async-done(((f32[128,48]{1,0:T(8,128)}), f32[32,48]{1,0:T(8,128)}) %reduce-scatter.21.cloned.1.call-update) | async-done | bytes 6160
  971.6 19.7 %all-reduce.30.cloned.1.call-done = f32[256,1024]{1,0:T(8,128)} async-done(((f32[256,1024]{1,0:T(8,128)}), f32[256,1024]{1,0:T(8,128)}) %all-reduce.30.cloned.1.call-update) | async-done | bytes 1048592 | tf_op jit(solution)/shard_map/psum | solution.py:334
  993.1 19.0 %all-reduce.21 = (f32[1024]{0:T(1024)S(1)}, f32[128]{0:T(128)S(1)}, f32[1024]{0:T(1024)S(1)}, f32[4,6]{1,0:T(4,128)S(1)}) all-reduce(f32[1024]{0:T(1024)S(1)} %get-tuple-element.993, f32[128]{0:T(128)S(1)} %multiply_reduce_fusion.10, f32[1024]{0:T(1024)S(1)} %copy-done.116, ...), channel_id=2, replica_groups=mesh['fsdp'=4,'ctx'=4,'tp'=2] {'fsdp'}, use_global_device_ids=true, to_apply=%region_31.32.clone | all-reduce | flops 2200 | bytes 17600
  1012.3 2.4 psum.120
  1015.3 17.8 %all-reduce.19 = (f32[256]{0:T(256)}, f32[256,4]{0,1:T(4,128)}, f32[3,4,4,32]{3,2,1,0:T(4,128)}, f32[32]{0:T(128)}, f32[256]{0:T(256)}, /*index=5*/f32[1,6]{1,0:T(1,128)S(1)}) all-reduce(f32[256]{0:T(256)S(1)} %dynamic-slice.2, f32[256,4]{0,1:T(4,128)S(1)} %copy.747, ...), channel_id=1, replica_groups=mesh['fsdp'=4,'ctx'=4,'tp'=2] {'ctx'}, use_global_device_ids=true, to_apply=%region_32.33 | all-reduce | flops 3110 | bytes 24880 | tf_op jit(solution)/shard_map/psum | solution.py:351
  1036.2 103.1 %all-reduce.32.cloned.1.call-done = (f32[3,256,512]{1,2,0:T(8,128)}, f32[512,256]{1,0:T(8,128)}, f32[2,256,1408]{1,2,0:T(8,128)}, f32[1408,256]{1,0:T(8,128)}) async-done(((f32[3,256,512]{1,2,0:T(8,128)}, f32[512,256]{1,0:T(8,128)}, f32[2,256,1408]{1,2,0:T(8,128)}, f32[1408,256]{1,0:T(8,128)}), (f32[3,256,512]{1,2,0:T(8,128)}, f32[512,256]{1,0:T(8,128)}, f32[2,256,1408]{1,2,0:T(8,128)}, ...) | async-done | bytes 6422544 | tf_op jit(solution)/shard_map/psum | solution.py:351
  1139.3 3.5 copy.687
  (630 shorter events, 243.6 us)
Async XLA Ops:
  7.2 49.1 %copy-start.134 = (u32[32]{0:T(128)S(1)}, u32[32]{0:T(128)}, u32[]{:S(2)}) copy-start(u32[32]{0:T(128)} %constant.232) | copy-start | bytes 388
  7.2 16.1 %copy-start.140 = (s32[1,4]{1,0:T(1,128)S(1)}, s32[1,4]{1,0:T(1,128)}, u32[]{:S(2)}) copy-start(s32[1,4]{1,0:T(1,128)} %param.23) | copy-start | bytes 52
  7.2 16.5 %copy-start.119 = (bf16[3,4,4,32]{3,2,1,0:T(4,128)(2,1)S(1)}, bf16[3,4,4,32]{3,2,1,0:T(4,128)(2,1)}, u32[]{:S(2)}) copy-start(bf16[3,4,4,32]{3,2,1,0:T(4,128)(2,1)} %param.27) | copy-start | bytes 9220
  7.2 35.2 %copy-start.132 = (bf16[256,4]{0,1:T(4,128)(2,1)S(1)}, bf16[256,4]{0,1:T(4,128)(2,1)}, u32[]{:S(2)}) copy-start(bf16[256,4]{0,1:T(4,128)(2,1)} %param.26) | copy-start | bytes 6148
  7.2 50.3 %copy-start.141 = (bf16[32]{0:T(256)(128)(2,1)S(1)}, bf16[32]{0:T(256)(128)(2,1)}, u32[]{:S(2)}) copy-start(bf16[32]{0:T(256)(128)(2,1)} %param.28) | copy-start | bytes 196
  7.2 62.6 %copy-start.11 = (bf16[256,1024]{1,0:T(8,128)(2,1)S(1)}, bf16[256,1024]{1,0:T(8,128)(2,1)}, u32[]{:S(2)}) copy-start(bf16[256,1024]{1,0:T(8,128)(2,1)} %param.22) | copy-start | bytes 1572868
  7.3 74.5 %all-gather.7.cloned.1.call-start = ((), (), s32[]{:S(2)}) async-start(), calls=%async_computation.6 | async-start | bytes 3932160 | tf_op jit(solution)/shard_map/all_gather | solution.py:180
  8.0 204.4 %all-gather.9.cloned.1.call-start = ((), (), s32[]{:S(2)}) async-start(), calls=%async_computation.7 | async-start | bytes 1310720 | tf_op jit(solution)/shard_map/all_gather | solution.py:184
  8.7 228.6 %all-reduce.28.cloned.1.call-start = ((), (), s32[]{:S(2)}) async-start(), calls=%async_computation.8 | async-start | bytes 2097152 | tf_op jit(solution)/shard_map/psum | solution.py:258
  8.8 61.3 %copy-start.82 = (f32[128,128]{0,1:T(8,128)}, f32[128,128]{0,1:T(8,128)S(1)}, u32[]{:S(2)}) copy-start(f32[128,128]{0,1:T(8,128)S(1)} %fusion.204) | copy-start | bytes 196612
  10.7 74.1 %copy-start.106 = (f32[256]{0:T(256)}, f32[256]{0:T(256)S(1)}, u32[]{:S(2)}) copy-start(f32[256]{0:T(256)S(1)} %add_rsqrt_fusion.4) | copy-start | bytes 3076
  23.7 66.1 %copy-start.108 = (f32[256,1]{0,1:T(1,128)}, f32[256,1]{0,1:T(1,128)S(1)}, u32[]{:S(2)}) copy-start(f32[256,1]{0,1:T(1,128)S(1)} %get-tuple-element.1145) | copy-start | bytes 3076
  23.7 66.1 %copy-start.110 = (f32[256,1]{0,1:T(1,128)}, f32[256,1]{0,1:T(1,128)S(1)}, u32[]{:S(2)}) copy-start(f32[256,1]{0,1:T(1,128)S(1)} %get-tuple-element.1146) | copy-start | bytes 3076
  23.7 66.1 %copy-start.112 = (f32[256,1]{0,1:T(1,128)}, f32[256,1]{0,1:T(1,128)S(1)}, u32[]{:S(2)}) copy-start(f32[256,1]{0,1:T(1,128)S(1)} %get-tuple-element.1147) | copy-start | bytes 3076
  23.7 66.1 %copy-start.114 = (f32[256,1]{0,1:T(1,128)}, f32[256,1]{0,1:T(1,128)S(1)}, u32[]{:S(2)}) copy-start(f32[256,1]{0,1:T(1,128)S(1)} %get-tuple-element.1148) | copy-start | bytes 3076
  54.6 30.1 %copy-start.100 = (bf16[1024,4]{0,1:T(4,128)(2,1)}, bf16[1024,4]{0,1:T(4,128)(2,1)S(1)}, u32[]{:S(2)}) copy-start(bf16[1024,4]{0,1:T(4,128)(2,1)S(1)} %all_gather.28) | copy-start | bytes 24580
  56.1 13.6 %copy-start.125 = (f32[4,64]{1,0:T(4,128)}, f32[4,64]{1,0:T(4,128)S(1)}, u32[]{:S(2)}) copy-start(f32[4,64]{1,0:T(4,128)S(1)} %convert_element_type.126) | copy-start | bytes 3076
  69.7 20.1 %copy-start.84 = (f32[3,512]{1,0:T(4,128)}, f32[3,512]{1,0:T(4,128)S(1)}, u32[]{:S(2)}) copy-start(f32[3,512]{1,0:T(4,128)S(1)} %get-tuple-element.1158) | copy-start | bytes 18436
  70.2 18.1 %copy-start.117 = (f32[256,4]{0,1:T(4,128)}, f32[256,4]{0,1:T(4,128)S(1)}, u32[]{:S(2)}) copy-start(f32[256,4]{0,1:T(4,128)S(1)} %fusion.116) | copy-start | bytes 12292
  84.8 4.8 collective-permute-start
  88.3 10.2 copy-start.28
  98.5 12.1 %copy-start.5 = (f32[4,4,64,64]{2,3,1,0:T(8,128)}, f32[4,4,64,64]{2,3,1,0:T(8,128)S(1)}, u32[]{:S(2)}) copy-start(f32[4,4,64,64]{2,3,1,0:T(8,128)S(1)} %fusion.243) | copy-start | bytes 786436
  107.5 41.4 %copy-start.94 = (f32[256,4]{0,1:T(4,128)}, f32[256,4]{0,1:T(4,128)S(1)}, u32[]{:S(2)}) copy-start(f32[256,4]{0,1:T(4,128)S(1)} %fusion.147) | copy-start | bytes 12292
  141.0 13.0 %copy-start.4 = (f32[4,4,128,128]{2,3,1,0:T(8,128)}, f32[4,4,128,128]{2,3,1,0:T(8,128)S(1)}, u32[]{:S(2)}) copy-start(f32[4,4,128,128]{2,3,1,0:T(8,128)S(1)} %get-tuple-element.1647) | copy-start | bytes 3145732
  143.0 10.3 copy-start.63
  143.0 15.4 %copy-start.18 = (f32[4,4,64,256]{3,2,1,0:T(8,128)S(1)}, f32[4,4,64,256]{3,2,1,0:T(8,128)}, u32[]{:S(2)}) copy-start(f32[4,4,64,256]{3,2,1,0:T(8,128)} %copy-done.17) | copy-start | bytes 3145732
  144.7 8.6 collective-permute-start.1
  148.9 10.4 copy-start.88
  154.0 8.3 collective-permute-start.2
  162.9 9.0 collective-permute-start.3
  207.3 5.1 copy-start.2
  215.1 131.6 %all-gather.11.cloned.1.call-start = ((), (), s32[]{:S(2)}) async-start(), calls=%async_computation.9 | async-start | bytes 7208960 | tf_op jit(solution)/shard_map/all_gather | solution.py:186
  215.7 190.0 %all-gather.13.cloned.1.call-start = ((), (), s32[]{:S(2)}) async-start(), calls=%async_computation.10 | async-start | bytes 3604480 | tf_op jit(solution)/shard_map/all_gather | solution.py:187
  216.3 218.2 %all-reduce.34.cloned.1.call-start = ((), (), s32[]{:S(2)}) async-start(), calls=%async_computation.19 | async-start | bytes 4194304 | tf_op jit(solution)/shard_map/psum | solution.py:270
  239.0 113.7 %copy-start.122 = (f32[256]{0:T(256)}, f32[256]{0:T(256)S(1)}, u32[]{:S(2)}) copy-start(f32[256]{0:T(256)S(1)} %get-tuple-element.1115) | copy-start | bytes 3076
  239.0 199.4 %copy-start = (f32[256,1024]{1,0:T(8,128)}, f32[256,1024]{1,0:T(8,128)S(1)}, u32[]{:S(2)}) copy-start(f32[256,1024]{1,0:T(8,128)S(1)} %get-tuple-element.1116) | copy-start | bytes 3145732
  239.1 199.4 %copy-start.96 = (f32[256]{0:T(256)}, f32[256]{0:T(256)S(1)}, u32[]{:S(2)}) copy-start(f32[256]{0:T(256)S(1)} %add_rsqrt_fusion.3) | copy-start | bytes 3076
  405.7 6.4 copy-start.26
  414.9 218.8 %reduce-scatter.13.cloned.1.call-start = ((), (), s32[]{:S(2)}) async-start(), calls=%async_computation.13 | async-start | bytes 2621440 | tf_op jit(solution)/shard_map/reduce_scatter | solution.py:345
  447.6 186.1 %reduce-scatter.17.cloned.1.call-start = ((), (), s32[]{:S(2)}) async-start(), calls=%async_computation.15 | async-start | bytes 7208960 | tf_op jit(solution)/shard_map/reduce_scatter | solution.py:348
  472.3 23.8 %copy-start.64 = (f32[4,128,128]{2,1,0:T(8,128)S(1)}, f32[4,128,128]{2,1,0:T(8,128)}, u32[]{:S(2)}) copy-start(f32[4,128,128]{2,1,0:T(8,128)} %copy.641) | copy-start | bytes 786436
  472.3 26.2 %copy-start.73 = (bf16[256,1024]{1,0:T(8,128)(2,1)S(1)}, bf16[256,1024]{1,0:T(8,128)(2,1)}, u32[]{:S(2)}) copy-start(bf16[256,1024]{1,0:T(8,128)(2,1)} %param.33) | copy-start | bytes 1572868
  472.3 26.2 %copy-start.76 = (bf16[256,1408]{1,0:T(8,128)(2,1)S(1)}, bf16[256,1408]{1,0:T(8,128)(2,1)}, u32[]{:S(2)}) copy-start(bf16[256,1408]{1,0:T(8,128)(2,1)} %copy-done.75) | copy-start | bytes 2162692
  473.8 10.4 collective-permute-start.4
  485.5 10.6 collective-permute-start.5
  497.2 10.0 collective-permute-start.6
  502.0 225.1 %reduce-scatter.11.cloned.1.call-start = ((), (), s32[]{:S(2)}) async-start(), calls=%async_computation.12 | async-start | bytes 7864320 | tf_op jit(solution)/shard_map/reduce_scatter | solution.py:341
  513.9 51.5 %copy-start.105 = (f32[4,64]{1,0:T(4,128)S(1)}, f32[4,64]{1,0:T(4,128)}, u32[]{:S(2)}) copy-start(f32[4,64]{1,0:T(4,128)} %slice_bitcast_fusion.4) | copy-start | bytes 3076
  513.9 5.4 copy-start.3
  526.6 5.5 copy-start.3
  539.4 5.5 copy-start.3
  552.2 5.4 copy-start.3
  604.7 6.5 copy-start.12
  604.7 6.5 copy-start.107
  604.7 6.5 collective-permute-start.7
  614.9 309.9 %reduce-scatter.15.cloned.1.call-start = ((), (), s32[]{:S(2)}) async-start(), calls=%async_computation.14 | async-start | bytes 14417920 | tf_op jit(solution)/shard_map/reduce_scatter | solution.py:347
  624.3 326.3 %reduce-scatter.19.cloned.1.call-start = ((), (), s32[]{:S(2)}) async-start(), calls=%async_computation.16 | async-start | bytes 655360
  627.6 343.0 %reduce-scatter.21.cloned.1.call-start = ((), (), s32[]{:S(2)}) async-start(), calls=%async_computation.17 | async-start | bytes 81920
  629.1 362.2 %all-reduce.30.cloned.1.call-start = ((), (), s32[]{:S(2)}) async-start(), calls=%async_computation.11 | async-start | bytes 2097152 | tf_op jit(solution)/shard_map/psum | solution.py:334
  633.6 505.7 %all-reduce.32.cloned.1.call-start = ((), (), s32[]{:S(2)}) async-start(), calls=%async_computation.18 | async-start | bytes 12845056 | tf_op jit(solution)/shard_map/psum | solution.py:351
  924.9 6.2 copy-start.53
  931.2 61.9 %copy-start.116 = (f32[1024]{0:T(1024)S(1)}, f32[1024]{0:T(1024)}, u32[]{:S(2)}) copy-start(f32[1024]{0:T(1024)} %get-tuple-element.998) | copy-start | bytes 12292
  931.2 103.7 %copy-start.21 = (f32[256,1024]{1,0:T(8,128)S(1)}, f32[256,1024]{1,0:T(8,128)}, u32[]{:S(2)}) copy-start(f32[256,1024]{1,0:T(8,128)} %copy-done.20) | copy-start | bytes 3145732
  991.3 43.6 %copy-start.65 = (f32[256,1024]{1,0:T(8,128)S(1)}, f32[256,1024]{1,0:T(8,128)}, u32[]{:S(2)}) copy-start(f32[256,1024]{1,0:T(8,128)} %all-reduce.30.cloned.1.call-done) | copy-start | bytes 3145732
  (104 other events, 217.4 us)
Sparse Core Ops, SparseCore 0:
  9.7 72.0 all-gather.6
  83.3 29.4 all-gather.8
  215.2 22.0 all-reduce.27
  238.8 107.8 all-gather.10
  348.3 57.4 all-gather.12
  415.0 19.4 all-reduce.33
  447.7 45.0 reduce-scatter.12
  502.1 105.3 reduce-scatter.16
  615.1 111.9 reduce-scatter.10
  729.4 195.4 reduce-scatter.14
  927.8 22.6 reduce-scatter.18
  953.3 17.2 reduce-scatter.20
  973.5 17.7 all-reduce.29
  995.5 143.7 all-reduce.31
where the time goes:
time: 1160 us; the launch traced here: 1150 us
  waiting for transfers between devices  684 us (59%)
  matrix products  210 us (18%)
  blocking collectives  103 us (9%)
  local copies, waits for them, and re-layouts  84.7 us (7%)
  other arithmetic  28.9 us (2%)
  starting transfers between devices  24 us (2%)
  between operations  19.1 us (2%)
    reduce_scatter x1, waiting for transfers between devices, local(): lax.psum_scatter(gate_up_grad, 'fsdp', scatter_dimension=1, tiled=True)  198 us
    dot_general x123, matrix products, product(): return jnp.einsum(form, left, right, precision=PRECISE)  163 us
    all_gather x1, waiting for transfers between devices, local(): lax.all_gather(gate_up_weight, 'fsdp', axis=1, tiled=True)  108 us
    psum x1, waiting for transfers between devices, local(): lax.psum((shares[0], shares[1], shares[2], shares[3], shares[4], shares[5...  103 us
    reduce_scatter x1, waiting for transfers between devices, local(): lax.psum_scatter(qkv_grad, 'fsdp', scatter_dimension=1, tiled=True)  93.4 us
    all_gather x1, waiting for transfers between devices, local(): lax.all_gather(down_weight, 'fsdp', axis=1, tiled=True)  53 us
    unnamed x16, waiting for transfers between devices  40.8 us
    ppermute x8, waiting for transfers between devices, passed_along(): lax.ppermute(value, axis, [(source, source + steps) for source in range(l...  34.1 us
  transfers between devices with their start and end apart: 22, of which 18 were waited for; matrix products, arithmetic and copies ran while one was open for 25% of the time, Pallas kernels for 0%

commit v1 on v0

--- a/solution.py
+++ b/solution.py
@@ -9,6 +9,16 @@
 CONV = 4
 PRECISE = lax.Precision.HIGHEST
 NORM_EPS = 1e-06
+
+
+def gather_around(x, axis, dim):
+    ways, here, turn = (lax.axis_size(axis), lax.axis_index(axis), x.shape[dim])
+    dims = [n * ways if d == dim else n for d, n in enumerate(x.shape)]
+    full = lax.dynamic_update_slice_in_dim(jnp.zeros(dims, x.dtype), x, here * turn, axis=dim)
+    for far in range(1, ways):
+        x = lax.ppermute(x, axis, [(d, (d + 1) % ways) for d in range(ways)])
+        full = lax.dynamic_update_slice_in_dim(full, x, (here - far) % ways * turn, axis=dim)
+    return full
 
 
 def passed_along(value, axis, steps):
@@ -184,7 +194,7 @@
         lax.all_gather(out_weight, "fsdp", axis=1, tiled=True),
         lax.all_gather(mlp_gain, "fsdp", axis=0, tiled=True),
         lax.all_gather(gate_up_weight, "fsdp", axis=1, tiled=True),
-        lax.all_gather(down_weight, "fsdp", axis=1, tiled=True),
+        gather_around(down_weight, "fsdp", 1),
     )
     (
         first_gain,

time: 1160 us -> 1120 us (0.966)
  waiting for transfers between devices: 684 us -> 627 us
    all_gather x1 -> x0, waiting for transfers between devices: 53 us -> none  [local(): lax.all_gather(down_weight, 'fsdp', axis=1, tiled=True)]
    ppermute x0 -> x3, waiting for transfers between devices: none -> 41.2 us  [gather_around(): x = lax.ppermute(x, axis, [(d, (d + 1) % ways) for d in range(ways)])]
    all_gather x1, waiting for transfers between devices: 108 us -> 72.2 us  [local(): lax.all_gather(gate_up_weight, 'fsdp', axis=1, tiled=True)]
    unnamed x16 -> x15, waiting for transfers between devices: 40.8 us -> 40.2 us
    unnamed x311 -> x313, local copies, waits for them, and re-layouts: 29.3 us -> 29.6 us
  transfers between devices with their start and end apart: 22 -> 24, of which waited for: 18 -> 18; matrix products, arithmetic and copies ran while one was open for 25% -> 26% of each run, Pallas kernels for 0% -> 0%
where the time goes in v1:
time: 1120 us
  waiting for transfers between devices  627 us (56%)
  matrix products  210 us (19%)
  blocking collectives  110 us (10%)
  local copies, waits for them, and re-layouts  93 us (8%)
  other arithmetic  29.4 us (3%)
  starting transfers between devices  26 us (2%)
  between operations  19.2 us (2%)
    reduce_scatter x1, waiting for transfers between devices, local(): lax.psum_scatter(gate_up_grad, 'fsdp', scatter_dimension=1, tiled=True)  198 us
    dot_general x123, matrix products, product(): return jnp.einsum(form, left, right, precision=PRECISE)  163 us
    psum x1, waiting for transfers between devices, local(): lax.psum((shares[0], shares[1], shares[2], shares[3], shares[4], shares[5...  103 us
    reduce_scatter x1, waiting for transfers between devices, local(): lax.psum_scatter(qkv_grad, 'fsdp', scatter_dimension=1, tiled=True)  93.8 us
    all_gather x1, waiting for transfers between devices, local(): lax.all_gather(gate_up_weight, 'fsdp', axis=1, tiled=True)  72.2 us
    ppermute x3, waiting for transfers between devices, gather_around(): x = lax.ppermute(x, axis, [(d, (d + 1) % ways) for d in range(ways)])  41.2 us
    unnamed x15, waiting for transfers between devices  40.2 us
    ppermute x8, waiting for transfers between devices, passed_along(): lax.ppermute(value, axis, [(source, source + steps) for source in range(l...  34.1 us
  transfers between devices with their start and end apart: 24, of which 18 were waited for; matrix products, arithmetic and copies ran while one was open for 26% of the time, Pallas kernels for 0%

profile of v1, /device:TPU:0, one launch (start us, length us, event | category | flops | bytes accessed | tf_op | source)
XLA Modules:
  0.0 1115.4 jit_solution(15911187758195093619)
XLA Ops:
  11.7 12.6 %all-gather = bf16[4,1,256]{2,1,0:T(2,128)(2,1)S(1)} all-gather(bf16[1,1,256]{2,1,0:T(2,128)(2,1)S(1)} %reshape.331), channel_id=1, replica_groups=mesh['fsdp'=4,'ctx'=4,'tp'=2] {'fsdp'}, dimensions={0}, use_global_device_ids=true | all-gather | bytes 2560 | tf_op jit(solution)/shard_map/all_gather | solution.py:189
  24.5 17.8 %all_gather.27 = bf16[3,4,4,128]{2,1,0,3:T(4,128)(2,1)S(1)} all-gather(bf16[3,4,4,32]{2,1,0,3:T(4,128)(2,1)S(1)} %copy.589), channel_id=1, replica_groups=mesh['fsdp'=4,'ctx'=4,'tp'=2] {'fsdp'}, dimensions={3}, use_global_device_ids=true | all-gather | bytes 15360 | tf_op jit(solution)/shard_map/all_gather | solution.py:192
  42.9 12.1 %all_gather.25 = bf16[1024,4]{0,1:T(4,128)(2,1)S(1)} all-gather(bf16[256,4]{0,1:T(4,128)(2,1)S(1)} %copy-done.133), channel_id=1, replica_groups=mesh['fsdp'=4,'ctx'=4,'tp'=2] {'fsdp'}, dimensions={0}, use_global_device_ids=true | all-gather | bytes 10240 | tf_op jit(solution)/shard_map/all_gather | solution.py:191
  58.2 10.9 all-reduce.14
  70.1 11.9 %all-gather.6.cloned.1.call-done = bf16[3,1024,512]{2,1,0:T(8,128)(2,1)} async-done(((bf16[3,256,512]{2,1,0:T(8,128)(2,1)}), bf16[3,1024,512]{2,1,0:T(8,128)(2,1)}) %all-gather.6.cloned.1.call-update) | async-done | bytes 3145744 | tf_op jit(solution)/shard_map/all_gather | solution.py:190
  82.0 2.9 convolution_convert_fusion
  85.0 3.4 collective-permute-start
  90.0 2.9 fusion.96
  92.9 2.9 reshape.310
  95.8 2.1 fusion.237
  107.6 2.0 copy.603
  118.7 2.5 convolution_bitcast_fusion.12
  121.2 2.5 copy.609
  123.7 2.0 fusion.101
  127.4 13.8 %while.85 = (s32[]{:T(128)}, f32[4,128,128]{1,2,0:T(8,128)S(1)}, f32[4,128,128]{1,2,0:T(8,128)}, f32[4,4,128,128]{2,3,1,0:T(8,128)S(1)}, f32[4,4,128,128]{2,3,1,0:T(8,128)}, /*index=5*/s32[]{:T(128)}, s32[]{:T(128)}) while((s32[]{:T(128)}, f32[4,128,128]{1,2,0:T(8,128)S(1)}, f32[4,128,128]{1,2,0:T(8,128)}, ...), condition=%wide.region_7.8_spmd.clone, body=%wide.region_6.7_spmd.clone.sunk | while | flops 201457664 | bytes 2884699 | solution.py:250
  128.4 2.0 fusion.424
  131.8 2.0 fusion.424
  135.2 2.0 fusion.424
  138.7 2.0 fusion.424
  144.9 4.2 collective-permute-start.1
  150.4 3.3 collective-permute-done.1
  154.3 4.4 collective-permute-start.2
  159.7 2.9 collective-permute-done.2
  163.3 5.9 collective-permute-start.3
  174.2 33.3 %while.82 = (s32[]{:T(128)}, f32[4,128,128]{1,2,0:T(8,128)}, f32[4,4,64,128]{3,2,1,0:T(8,128)}, f32[4,4,128,128]{2,3,1,0:T(8,128)S(1)}, f32[4,1,64,1]{2,3,1,0:T(...) while((s32[]{:T(128)}, f32[4,128,128]{1,2,0:T(8,128)}, ...), condition=%wide.region_10.11_spmd, body=%wide.region_9.10_spmd.sunk | while | flops 226689024 | bytes 3937937 | solution.py:152
  180.4 2.1 fusion.401
  188.8 2.1 fusion.401
  197.1 2.1 fusion.401
  205.4 2.1 fusion.401
  212.6 2.7 fusion.248
  216.5 16.7 %collective-permute-done.4 = bf16[1408,256]{1,0:T(8,128)(2,1)} collective-permute-done((bf16[1408,256]{1,0:T(8,128)(2,1)S(1)}, bf16[1408,256]{1,0:T(8,128)(2,1)}, u32[]{:S(2)}, u32[]{:S(2)}) %collective-permute-start.4) | collective-permute-done | bytes 720928 | tf_op jit(solution)/shard_map/ppermute | solution.py:19
  233.8 17.2 %all-gather.1 = bf16[4,1,256]{2,1,0:T(2,128)(2,1)S(1)} all-gather(bf16[1,1,256]{2,1,0:T(2,128)(2,1)S(1)} %reshape.333), channel_id=1, replica_groups=mesh['fsdp'=4,'ctx'=4,'tp'=2] {'fsdp'}, dimensions={0}, use_global_device_ids=true | all-gather | bytes 2560 | tf_op jit(solution)/shard_map/all_gather | solution.py:195
  261.1 24.5 %collective-permute-done.6 = bf16[1408,256]{1,0:T(8,128)(2,1)S(1)} collective-permute-done((bf16[1408,256]{1,0:T(8,128)(2,1)}, bf16[1408,256]{1,0:T(8,128)(2,1)S(1)}, u32[]{:S(2)}, u32[]{:S(2)}) %collective-permute-start.6) | collective-permute-done | bytes 720928 | tf_op jit(solution)/shard_map/ppermute | solution.py:19
  288.2 72.2 %all-gather.10.cloned.1.call-done = bf16[2,1024,1408]{2,1,0:T(8,128)(2,1)} async-done(((bf16[2,256,1408]{2,1,0:T(8,128)(2,1)}), bf16[2,1024,1408]{2,1,0:T(8,128)(2,1)}) %all-gather.10.cloned.1.call-update) | async-done | bytes 5767184 | tf_op jit(solution)/shard_map/all_gather | solution.py:196
  360.5 4.5 fusion.207
  365.0 3.4 fusion.133
  368.4 4.5 fusion.249
  373.0 2.7 convolution_bitcast_fusion.13
  375.8 2.8 while.83
  382.5 13.0 %all-reduce.34.cloned.1.call-done = (f32[256,1024]{1,0:T(8,128)}, f32[256,1024]{1,0:T(8,128)}) async-done(((f32[256,1024]{1,0:T(8,128)}, f32[256,1024]{1,0:T(8,128)}), (f32[256,1024]{1,0:T(8,128)}, f32[256,1024]{1,0:T(8,128)})) %all-reduce.34.cloned.1.call-update) | async-done | bytes 2097168 | tf_op jit(solution)/shard_map/psum | solution.py:280
  395.5 3.9 multiply_reduce_fusion.4
  402.6 2.0 fusion.226
  409.5 21.9 %while.86 = (s32[]{:T(128)}, f32[4,128,128]{1,2,0:T(8,128)}, f32[4,4,128,128]{3,2,1,0:T(8,128)}, f32[4,1,64,1]{2,3,1,0:T(1,128)S(1)}, f32[4,4,64,128]{3,2,1,0:T(...) while((s32[]{:T(128)}, f32[4,128,128]{1,2,0:T(8,128)}, ...), condition=%wide.region_21.22_spmd.clone, body=%wide.region_20.21_spmd.clone.sunk | while | flops 226787328 | bytes 2756239 | solution.py:152
  435.9 9.1 collective-permute-done.7
  447.7 9.2 collective-permute-done.8
  459.3 3.5 fusion.195
  462.8 5.0 collective-permute-done.9
  474.6 51.4 %while.84 = (s32[]{:T(128)}, f32[4,128,128]{1,2,0:T(8,128)S(1)}, f32[4,4,64,128]{3,2,0,1:T(8,128)}, f32[4,4,64,128]{3,2,0,1:T(8,128)}, f32[4,4,64,64]{2,3,1,0:T(...) while((s32[]{:T(128)}, f32[4,128,128]{1,2,0:T(8,128)S(1)}, ...), condition=%wide.region_23.24_spmd, body=%wide.region_22.23_spmd.sunk | while | flops 453312512 | bytes 9840861 | solution.py:152
  555.3 2.1 fusion.126
  567.6 4.2 collective-permute-done.10
  571.8 3.7 convolution_bitcast_fusion.10
  576.8 8.1 convolution_bitcast_fusion.9
  590.1 4.2 fusion.102
  594.4 93.8 %reduce-scatter.11.cloned.1.call-done = f32[3,256,512]{1,2,0:T(8,128)} async-done(((f32[3,1024,512]{1,2,0:T(8,128)}), f32[3,256,512]{1,2,0:T(8,128)}) %reduce-scatter.11.cloned.1.call-update) | async-done | bytes 1572880 | tf_op jit(solution)/shard_map/reduce_scatter | solution.py:351
  688.1 197.9 %reduce-scatter.15.cloned.1.call-done = f32[2,256,1408]{1,2,0:T(8,128)} async-done(((f32[2,1024,1408]{1,2,0:T(8,128)}), f32[2,256,1408]{1,2,0:T(8,128)}) %reduce-scatter.15.cloned.1.call-update) | async-done | bytes 2883600 | tf_op jit(solution)/shard_map/reduce_scatter | solution.py:357
  888.4 4.0 stack.42
  892.6 18.9 %reduce-scatter.19.cloned.1.call-done = f32[256,4]{1,0:T(8,128)} async-done(((f32[1024,4]{1,0:T(8,128)}), f32[256,4]{1,0:T(8,128)}) %reduce-scatter.19.cloned.1.call-update) | async-done | bytes 4112
  912.6 19.2 %reduce-scatter.21.cloned.1.call-done = f32[32,48]{1,0:T(8,128)} async-done(((f32[128,48]{1,0:T(8,128)}), f32[32,48]{1,0:T(8,128)}) %reduce-scatter.21.cloned.1.call-update) | async-done | bytes 6160
  932.8 19.6 %all-reduce.30.cloned.1.call-done = f32[256,1024]{1,0:T(8,128)} async-done(((f32[256,1024]{1,0:T(8,128)}), f32[256,1024]{1,0:T(8,128)}) %all-reduce.30.cloned.1.call-update) | async-done | bytes 1048592 | tf_op jit(solution)/shard_map/psum | solution.py:344
  954.1 19.0 %all-reduce.21 = (f32[1024]{0:T(1024)S(1)}, f32[128]{0:T(128)S(1)}, f32[1024]{0:T(1024)S(1)}, f32[4,6]{1,0:T(4,128)S(1)}) all-reduce(f32[1024]{0:T(1024)S(1)} %get-tuple-element.993, f32[128]{0:T(128)S(1)} %multiply_reduce_fusion.10, f32[1024]{0:T(1024)S(1)} %copy-done.117, ...), channel_id=2, replica_groups=mesh['fsdp'=4,'ctx'=4,'tp'=2] {'fsdp'}, use_global_device_ids=true, to_apply=%region_31.32.clone | all-reduce | flops 2200 | bytes 17600
  973.3 2.4 psum.120
  976.4 17.8 %all-reduce.19 = (f32[256]{0:T(256)}, f32[256,4]{0,1:T(4,128)}, f32[3,4,4,32]{3,2,1,0:T(4,128)}, f32[32]{0:T(128)}, f32[256]{0:T(256)}, /*index=5*/f32[1,6]{1,0:T(1,128)S(1)}) all-reduce(f32[256]{0:T(256)S(1)} %dynamic-slice.2, f32[256,4]{0,1:T(4,128)S(1)} %copy.747, ...), channel_id=1, replica_groups=mesh['fsdp'=4,'ctx'=4,'tp'=2] {'ctx'}, use_global_device_ids=true, to_apply=%region_32.33 | all-reduce | flops 3110 | bytes 24880 | tf_op jit(solution)/shard_map/psum | solution.py:361
  997.3 103.2 %all-reduce.32.cloned.1.call-done = (f32[3,256,512]{1,2,0:T(8,128)}, f32[512,256]{1,0:T(8,128)}, f32[2,256,1408]{1,2,0:T(8,128)}, f32[1408,256]{1,0:T(8,128)}) async-done(((f32[3,256,512]{1,2,0:T(8,128)}, f32[512,256]{1,0:T(8,128)}, f32[2,256,1408]{1,2,0:T(8,128)}, f32[1408,256]{1,0:T(8,128)}), (f32[3,256,512]{1,2,0:T(8,128)}, f32[512,256]{1,0:T(8,128)}, f32[2,256,1408]{1,2,0:T(8,128)}, ...) | async-done | bytes 6422544 | tf_op jit(solution)/shard_map/psum | solution.py:361
  1100.5 3.5 copy.687
  (641 shorter events, 253.5 us)
Async XLA Ops:
  7.2 49.4 %copy-start.135 = (u32[32]{0:T(128)S(1)}, u32[32]{0:T(128)}, u32[]{:S(2)}) copy-start(u32[32]{0:T(128)} %constant.266) | copy-start | bytes 388
  7.2 17.1 %copy-start.120 = (bf16[3,4,4,32]{3,2,1,0:T(4,128)(2,1)S(1)}, bf16[3,4,4,32]{3,2,1,0:T(4,128)(2,1)}, u32[]{:S(2)}) copy-start(bf16[3,4,4,32]{3,2,1,0:T(4,128)(2,1)} %param.27) | copy-start | bytes 9220
  7.2 35.7 %copy-start.133 = (bf16[256,4]{0,1:T(4,128)(2,1)S(1)}, bf16[256,4]{0,1:T(4,128)(2,1)}, u32[]{:S(2)}) copy-start(bf16[256,4]{0,1:T(4,128)(2,1)} %param.26) | copy-start | bytes 6148
  7.2 50.7 %copy-start.140 = (bf16[32]{0:T(256)(128)(2,1)S(1)}, bf16[32]{0:T(256)(128)(2,1)}, u32[]{:S(2)}) copy-start(bf16[32]{0:T(256)(128)(2,1)} %param.28) | copy-start | bytes 196
  7.2 62.5 %copy-start.11 = (bf16[256,1024]{1,0:T(8,128)(2,1)S(1)}, bf16[256,1024]{1,0:T(8,128)(2,1)}, u32[]{:S(2)}) copy-start(bf16[256,1024]{1,0:T(8,128)(2,1)} %param.22) | copy-start | bytes 1572868
  7.2 74.7 %all-gather.6.cloned.1.call-start = ((), (), s32[]{:S(2)}) async-start(), calls=%async_computation.6 | async-start | bytes 3932160 | tf_op jit(solution)/shard_map/all_gather | solution.py:190
  8.0 204.7 %all-gather.8.cloned.1.call-start = ((), (), s32[]{:S(2)}) async-start(), calls=%async_computation.7 | async-start | bytes 1310720 | tf_op jit(solution)/shard_map/all_gather | solution.py:194
  8.7 277.7 %all-reduce.28.cloned.1.call-start = ((), (), s32[]{:S(2)}) async-start(), calls=%async_computation.8 | async-start | bytes 2097152 | tf_op jit(solution)/shard_map/psum | solution.py:268
  8.8 61.2 %copy-start.83 = (f32[128,128]{0,1:T(8,128)}, f32[128,128]{0,1:T(8,128)S(1)}, u32[]{:S(2)}) copy-start(f32[128,128]{0,1:T(8,128)S(1)} %fusion.204) | copy-start | bytes 196612
  9.7 32.9 %copy-start.137 = (s32[4,1]{0,1:T(1,128)}, s32[4,1]{0,1:T(1,128)S(1)}, u32[]{:S(2)}) copy-start(s32[4,1]{0,1:T(1,128)S(1)} %reduce-window.4) | copy-start | bytes 52
  9.9 80.1 %copy-start.109 = (f32[256,1]{0,1:T(1,128)}, f32[256,1]{0,1:T(1,128)S(1)}, u32[]{:S(2)}) copy-start(f32[256,1]{0,1:T(1,128)S(1)} %get-tuple-element.1145) | copy-start | bytes 3076
  9.9 80.1 %copy-start.111 = (f32[256,1]{0,1:T(1,128)}, f32[256,1]{0,1:T(1,128)S(1)}, u32[]{:S(2)}) copy-start(f32[256,1]{0,1:T(1,128)S(1)} %get-tuple-element.1146) | copy-start | bytes 3076
  9.9 80.1 %copy-start.113 = (f32[256,1]{0,1:T(1,128)}, f32[256,1]{0,1:T(1,128)S(1)}, u32[]{:S(2)}) copy-start(f32[256,1]{0,1:T(1,128)S(1)} %get-tuple-element.1147) | copy-start | bytes 3076
  9.9 80.1 %copy-start.115 = (f32[256,1]{0,1:T(1,128)}, f32[256,1]{0,1:T(1,128)S(1)}, u32[]{:S(2)}) copy-start(f32[256,1]{0,1:T(1,128)S(1)} %get-tuple-element.1148) | copy-start | bytes 3076
  11.7 73.3 %copy-start.107 = (f32[256]{0:T(256)}, f32[256]{0:T(256)S(1)}, u32[]{:S(2)}) copy-start(f32[256]{0:T(256)S(1)} %add_rsqrt_fusion.4) | copy-start | bytes 3076
  55.0 29.9 %copy-start.101 = (bf16[1024,4]{0,1:T(4,128)(2,1)}, bf16[1024,4]{0,1:T(4,128)(2,1)S(1)}, u32[]{:S(2)}) copy-start(bf16[1024,4]{0,1:T(4,128)(2,1)S(1)} %all_gather.25) | copy-start | bytes 24580
  56.4 13.2 %copy-start.126 = (f32[4,64]{1,0:T(4,128)}, f32[4,64]{1,0:T(4,128)S(1)}, u32[]{:S(2)}) copy-start(f32[4,64]{1,0:T(4,128)S(1)} %convert_element_type.126) | copy-start | bytes 3076
  69.6 20.4 %copy-start.85 = (f32[3,512]{1,0:T(4,128)}, f32[3,512]{1,0:T(4,128)S(1)}, u32[]{:S(2)}) copy-start(f32[3,512]{1,0:T(4,128)S(1)} %get-tuple-element.1158) | copy-start | bytes 18436
  70.1 18.5 %copy-start.118 = (f32[256,4]{0,1:T(4,128)}, f32[256,4]{0,1:T(4,128)S(1)}, u32[]{:S(2)}) copy-start(f32[256,4]{0,1:T(4,128)S(1)} %fusion.116) | copy-start | bytes 12292
  85.0 4.8 collective-permute-start
  88.5 10.1 copy-start.27
  98.6 12.1 %copy-start.5 = (f32[4,4,64,64]{2,3,1,0:T(8,128)}, f32[4,4,64,64]{2,3,1,0:T(8,128)S(1)}, u32[]{:S(2)}) copy-start(f32[4,4,64,64]{2,3,1,0:T(8,128)S(1)} %fusion.243) | copy-start | bytes 786436
  107.6 41.4 %copy-start.95 = (f32[256,4]{0,1:T(4,128)}, f32[256,4]{0,1:T(4,128)S(1)}, u32[]{:S(2)}) copy-start(f32[256,4]{0,1:T(4,128)S(1)} %fusion.147) | copy-start | bytes 12292
  141.2 13.2 %copy-start.4 = (f32[4,4,128,128]{2,3,1,0:T(8,128)}, f32[4,4,128,128]{2,3,1,0:T(8,128)S(1)}, u32[]{:S(2)}) copy-start(f32[4,4,128,128]{2,3,1,0:T(8,128)S(1)} %get-tuple-element.1646) | copy-start | bytes 3145732
  143.1 10.5 copy-start.62
  143.1 15.6 %copy-start.18 = (f32[4,4,64,256]{3,2,1,0:T(8,128)S(1)}, f32[4,4,64,256]{3,2,1,0:T(8,128)}, u32[]{:S(2)}) copy-start(f32[4,4,64,256]{3,2,1,0:T(8,128)} %copy-done.17) | copy-start | bytes 3145732
  144.9 8.8 collective-permute-start.1
  149.1 10.6 copy-start.89
  154.3 8.3 collective-permute-start.2
  163.3 9.1 collective-permute-start.3
  215.4 17.9 %copy-start.138 = (s32[4,1]{0,1:T(1,128)S(1)}, s32[4,1]{0,1:T(1,128)}, u32[]{:S(2)}) copy-start(s32[4,1]{0,1:T(1,128)} %copy-done.137) | copy-start | bytes 52
  215.4 18.4 %copy-start.141 = (bf16[256]{0:T(256)(128)(2,1)S(1)}, bf16[256]{0:T(256)(128)(2,1)}, u32[]{:S(2)}) copy-start(bf16[256]{0:T(256)(128)(2,1)} %param.30) | copy-start | bytes 1540
  215.4 145.0 %all-gather.10.cloned.1.call-start = ((), (), s32[]{:S(2)}) async-start(), calls=%async_computation.9 | async-start | bytes 7208960 | tf_op jit(solution)/shard_map/all_gather | solution.py:196
  216.0 179.5 %all-reduce.34.cloned.1.call-start = ((), (), s32[]{:S(2)}) async-start(), calls=%async_computation.18 | async-start | bytes 4194304 | tf_op jit(solution)/shard_map/psum | solution.py:280
  216.5 16.8 %collective-permute-start.4 = (bf16[1408,256]{1,0:T(8,128)(2,1)S(1)}, bf16[1408,256]{1,0:T(8,128)(2,1)}, u32[]{:S(2)}, u32[]{:S(2)}) collective-permute-start(bf16[1408,256]{1,0:T(8,128)(2,1)S(1)} %copy-done.80), channel_id=1, source_target_pairs={{0,8},{8,16},{16,24},{24,0},{1,9},{9,17},{17,25},{25,1},{2,10},{10... | collective-permute-start | bytes 2162696 | tf_op jit(solution)/shard_map/ppermute | solution.py:19
  233.2 19.0 %collective-permute-start.5 = (bf16[1408,256]{1,0:T(8,128)(2,1)}, bf16[1408,256]{1,0:T(8,128)(2,1)}, u32[]{:S(2)}, u32[]{:S(2)}) collective-permute-start(bf16[1408,256]{1,0:T(8,128)(2,1)} %collective-permute-done.4), channel_id=1, source_target_pairs={{0,8},{8,16},{16,24},{24,0},{1,9},{9,17},{17,25},{25,1},{2,10},{10... | collective-permute-start | bytes 2162696 | tf_op jit(solution)/shard_map/ppermute | solution.py:19
  252.2 33.4 %collective-permute-start.6 = (bf16[1408,256]{1,0:T(8,128)(2,1)}, bf16[1408,256]{1,0:T(8,128)(2,1)S(1)}, u32[]{:S(2)}, u32[]{:S(2)}) collective-permute-start(bf16[1408,256]{1,0:T(8,128)(2,1)} %collective-permute-done.5), channel_id=1, source_target_pairs={{0,8},{8,16},{16,24},{24,0},{1,9},{9,17},{17,25},{25,1},{2,10},{10... | collective-permute-start | bytes 2162696 | tf_op jit(solution)/shard_map/ppermute | solution.py:19
  288.2 76.8 %copy-start.123 = (f32[256]{0:T(256)}, f32[256]{0:T(256)S(1)}, u32[]{:S(2)}) copy-start(f32[256]{0:T(256)S(1)} %get-tuple-element.1115) | copy-start | bytes 3076
  288.2 111.2 %copy-start = (f32[256,1024]{1,0:T(8,128)}, f32[256,1024]{1,0:T(8,128)S(1)}, u32[]{:S(2)}) copy-start(f32[256,1024]{1,0:T(8,128)S(1)} %get-tuple-element.1116) | copy-start | bytes 3145732
  288.2 111.2 %copy-start.97 = (f32[256]{0:T(256)}, f32[256]{0:T(256)S(1)}, u32[]{:S(2)}) copy-start(f32[256]{0:T(256)S(1)} %add_rsqrt_fusion.3) | copy-start | bytes 3076
  360.4 12.5 %slice-start = ((s8[5767168]{0:T(1024)(128)(4,1)}), s8[4194304]{0:T(1024)(128)(4,1)S(1)}, s32[]{:S(2)}) async-start(s8[5767168]{0:T(1024)(128)(4,1)} %bitcast.592), calls=%async_computation.19 | async-start | bytes 8388608
  365.0 8.0 slice-start.1
  375.7 218.6 %reduce-scatter.13.cloned.1.call-start = ((), (), s32[]{:S(2)}) async-start(), calls=%async_computation.12 | async-start | bytes 2621440 | tf_op jit(solution)/shard_map/reduce_scatter | solution.py:355
  408.6 185.8 %reduce-scatter.17.cloned.1.call-start = ((), (), s32[]{:S(2)}) async-start(), calls=%async_computation.14 | async-start | bytes 7208960 | tf_op jit(solution)/shard_map/reduce_scatter | solution.py:358
  433.2 23.7 %copy-start.63 = (f32[4,128,128]{2,1,0:T(8,128)S(1)}, f32[4,128,128]{2,1,0:T(8,128)}, u32[]{:S(2)}) copy-start(f32[4,128,128]{2,1,0:T(8,128)} %copy.641) | copy-start | bytes 786436
  433.2 26.1 %copy-start.73 = (bf16[256,1024]{1,0:T(8,128)(2,1)S(1)}, bf16[256,1024]{1,0:T(8,128)(2,1)}, u32[]{:S(2)}) copy-start(bf16[256,1024]{1,0:T(8,128)(2,1)} %param.33) | copy-start | bytes 1572868
  433.2 26.1 %copy-start.76 = (bf16[256,1408]{1,0:T(8,128)(2,1)S(1)}, bf16[256,1408]{1,0:T(8,128)(2,1)}, u32[]{:S(2)}) copy-start(bf16[256,1408]{1,0:T(8,128)(2,1)} %copy-done.75) | copy-start | bytes 2162692
  434.6 10.4 collective-permute-start.7
  446.4 10.5 collective-permute-start.8
  458.0 9.9 collective-permute-start.9
  462.8 225.3 %reduce-scatter.11.cloned.1.call-start = ((), (), s32[]{:S(2)}) async-start(), calls=%async_computation.11 | async-start | bytes 7864320 | tf_op jit(solution)/shard_map/reduce_scatter | solution.py:351
  474.6 51.4 %copy-start.106 = (f32[4,64]{1,0:T(4,128)S(1)}, f32[4,64]{1,0:T(4,128)}, u32[]{:S(2)}) copy-start(f32[4,64]{1,0:T(4,128)} %slice_bitcast_fusion.4) | copy-start | bytes 3076
  565.3 6.5 copy-start.12
  565.3 6.5 copy-start.108
  565.3 6.5 collective-permute-start.10
  575.6 310.5 %reduce-scatter.15.cloned.1.call-start = ((), (), s32[]{:S(2)}) async-start(), calls=%async_computation.13 | async-start | bytes 14417920 | tf_op jit(solution)/shard_map/reduce_scatter | solution.py:357
  584.9 326.7 %reduce-scatter.19.cloned.1.call-start = ((), (), s32[]{:S(2)}) async-start(), calls=%async_computation.15 | async-start | bytes 655360
  588.3 343.5 %reduce-scatter.21.cloned.1.call-start = ((), (), s32[]{:S(2)}) async-start(), calls=%async_computation.16 | async-start | bytes 81920
  589.8 362.6 %all-reduce.30.cloned.1.call-start = ((), (), s32[]{:S(2)}) async-start(), calls=%async_computation.10 | async-start | bytes 2097152 | tf_op jit(solution)/shard_map/psum | solution.py:344
  594.3 506.3 %all-reduce.32.cloned.1.call-start = ((), (), s32[]{:S(2)}) async-start(), calls=%async_computation.17 | async-start | bytes 12845056 | tf_op jit(solution)/shard_map/psum | solution.py:361
  886.1 6.3 copy-start.52
  892.4 61.7 %copy-start.117 = (f32[1024]{0:T(1024)S(1)}, f32[1024]{0:T(1024)}, u32[]{:S(2)}) copy-start(f32[1024]{0:T(1024)} %get-tuple-element.998) | copy-start | bytes 12292
  892.4 103.6 %copy-start.21 = (f32[256,1024]{1,0:T(8,128)S(1)}, f32[256,1024]{1,0:T(8,128)}, u32[]{:S(2)}) copy-start(f32[256,1024]{1,0:T(8,128)} %copy-done.20) | copy-start | bytes 3145732
  952.4 43.7 %copy-start.64 = (f32[256,1024]{1,0:T(8,128)S(1)}, f32[256,1024]{1,0:T(8,128)}, u32[]{:S(2)}) copy-start(f32[256,1024]{1,0:T(8,128)} %all-reduce.30.cloned.1.call-done) | copy-start | bytes 3145732
  (107 other events, 250.8 us)
Sparse Core Ops, SparseCore 0:
  9.6 72.2 all-gather.5
  83.5 29.3 all-gather.7
  215.5 21.5 all-reduce.27
  238.6 121.7 all-gather.9
  375.8 19.5 all-reduce.33
  408.7 45.0 reduce-scatter.12
  462.9 105.5 reduce-scatter.16
  575.7 112.3 reduce-scatter.10
  690.6 195.4 reduce-scatter.14
  888.9 22.6 reduce-scatter.18
  914.5 17.2 reduce-scatter.20
  934.6 17.7 all-reduce.29
  956.7 143.7 all-reduce.31
